TPU v7x, 128 devices: a whole 4x4x4 slice. The times are simulated.
128 devices in a mesh: prompt: 4 (over z_hi, core), resp: 32 (over y, x, z_lo).
Axes of the slice: x: 4, y: 4, z: 4 (z_hi: 2, z_lo: 2; z = z_hi * 2 + z_lo), core: 2. Of those that a mesh axis runs over, the one named last changes fastest.
Arguments:
- queries: bfloat16 [4, 4096, 8192], P('prompt', 'resp'), may hold values from -6 to 6
- resp_kv: bfloat16 [4, 4096, 2048], P('prompt', 'resp'), may hold values from -6 to 6
- resp_segments: int32 [4, 4096], P('prompt', 'resp'), may hold values from 0 to 7, never falling along the last dimension, each value on 1 to 896 neighbouring positions
- prefix_kv: bfloat16 [512, 8, 2048], P(('prompt', 'resp')), may hold values from -6 to 6
- tile_plan: int32 [512, 2], P(('prompt', 'resp')), may hold values from 0 to 127, as said below
- prompt_lengths: int32 [4], P('prompt'), may hold values from 8 to 1024
Outputs:
- attended: bfloat16 [4, 4096, 8192], P('prompt', 'resp')
Inputs may be any that keep to these rules, and one draw needn't show every extreme that they name: `tile_plan`: column 0 is a group in 0 .. 3 and column 1 a place in 0 .. 127; each pair of group and place stands once; the 4 tiles of each device hold one tile of every group, in any order. `resp_segments`: response numbers never fall along a group's tokens; each response has 1 to 896 tokens.
All inputs are finite; a program needn't handle non-finite values.
Results may differ from a plain program's by a relative error of at most 0.0055.
Values may be sent and summed in bfloat16 or wider, within the bound.
A program may use at most 128 MiB of HBM per device.

v0:
```python
import math

import jax
import jax.numpy as jnp
from jax import lax
from jax.sharding import PartitionSpec as P

H = 64
KVH = 8
HD = 128


NEG_FILL = -1e30


def passed_along(value, axis, steps):
    count = lax.axis_size(axis)
    first, last = (max(0, -steps), min(count, count - steps))
    return lax.ppermute(value, axis, [(source, source + steps) for source in range(first, last)])


def absorb(carry, query_head_rows, key_vectors, value_vectors, visible, score_scale):
    running, total, weighted_sum = carry
    logit_scores = (
        jnp.einsum(
            "wcpo,lco->wcpl", query_head_rows, key_vectors, preferred_element_type=jnp.float32
        )
        * score_scale
    )
    logit_scores = jnp.where(visible, logit_scores, NEG_FILL)
    fresh = jnp.maximum(running, jnp.max(logit_scores, axis=-1))
    factor = jnp.exp(running - fresh)
    attention_weight = jnp.where(visible, jnp.exp(logit_scores - fresh[..., None]), 0.0)
    total = total * factor + jnp.sum(attention_weight, axis=-1)
    update = jnp.einsum(
        "luem,mut->luet",
        attention_weight.astype(jnp.bfloat16),
        value_vectors,
        preferred_element_type=jnp.float32,
    )
    weighted_sum = weighted_sum * factor[..., None] + update
    return (fresh, total, weighted_sum)


def on_device(queries, resp_kv, resp_segments, prefix_kv, tile_plan, prompt_lengths):
    rows = queries.shape[1]
    heads_kv = KVH
    width = HD
    group_size = H // KVH
    split = heads_kv * width
    score_scale = 1.0 / math.sqrt(width)
    reach = 7
    query_head_rows = queries[0].reshape(rows, heads_kv, group_size, width)
    own_kv = resp_kv[0]
    own_seg = resp_segments[0] + 1
    key_vectors = own_kv[:, :split].reshape(rows, heads_kv, width)
    value_vectors = own_kv[:, split:].reshape(rows, heads_kv, width)
    query_pos = jnp.arange(rows, dtype=jnp.int32)
    visible = (own_seg[None, :] == own_seg[:, None]) & (query_pos[None, :] <= query_pos[:, None])
    start_state = (
        jnp.full((rows, heads_kv, group_size), NEG_FILL, jnp.float32),
        jnp.zeros((rows, heads_kv, group_size), jnp.float32),
        jnp.zeros((rows, heads_kv, group_size, width), jnp.float32),
    )
    carry = absorb(
        start_state,
        query_head_rows,
        key_vectors,
        value_vectors,
        visible[:, None, None, :],
        score_scale,
    )
    moving = (own_kv, own_seg)
    for step in range(reach):
        moving = passed_along((moving[0], moving[1]), "resp", 1)
        block_kv = moving[0]
        seen = own_seg[:, None] == moving[1][None, :]

        def absorb_update(current):
            block_keys = block_kv[:, :split].reshape(-1, heads_kv, width)
            block_values = block_kv[:, split:].reshape(-1, heads_kv, width)
            return absorb(
                current,
                query_head_rows,
                block_keys,
                block_values,
                seen[:, None, None, :],
                score_scale,
            )

        carry = lax.cond(jnp.any(seen), absorb_update, lambda current: current, carry)
    group = lax.axis_index("prompt")
    limit = prompt_lengths[0]
    n_prompt = lax.axis_size("prompt")
    state = carry
    tiles = lax.all_gather(prefix_kv, ("prompt", "resp"), axis=0, tiled=True)
    plan = lax.all_gather(tile_plan, ("prompt", "resp"), axis=0, tiled=True)
    count = tiles.shape[0]
    tile = tiles.shape[1]
    count = count // n_prompt
    order = jnp.argsort(jnp.where(plan[:, 0] == group, 0, 1), stable=True)[:count]
    tiles = tiles[order]
    plan = plan[order]
    cap = max(1, 512 // tile)
    per = max((d for d in range(1, min(count, cap) + 1) if count % d == 0))
    places = plan[:, 1][:, None] * tile + jnp.arange(tile, dtype=jnp.int32)[None, :]
    live = (places < limit).reshape(count // per, per * tile)
    blocks = tiles.reshape(count // per, per * tile, tiles.shape[2])

    def advance(inner, item):
        block, mask = item

        def update(current):
            block_keys = block[:, :split].reshape(-1, heads_kv, width)
            block_values = block[:, split:].reshape(-1, heads_kv, width)
            return absorb(
                current,
                query_head_rows,
                block_keys,
                block_values,
                mask[None, None, None, :],
                score_scale,
            )

        return (lax.cond(jnp.any(mask), update, lambda current: current, inner), None)

    state, _ = lax.scan(advance, state, (blocks, live))
    carry = state
    running, total, weighted_sum = carry
    result = (weighted_sum / total[..., None]).reshape(rows, H * HD).astype(jnp.bfloat16)
    return result[None]


def solution(mesh):
    return jax.shard_map(
        on_device,
        mesh=mesh,
        in_specs=(
            P("prompt", "resp", None),
            P("prompt", "resp", None),
            P("prompt", "resp"),
            P(("prompt", "resp"), None, None),
            P(("prompt", "resp"), None),
            P("prompt"),
        ),
        out_specs=P("prompt", "resp", None),
        check_vma=False,
    )
```

profile of v0, /device:TPU:40, one launch (start us, length us, event | category | flops | bytes accessed | tf_op | source)
XLA Modules:
  0.0 582.0 jit_solution(3379956316032789623)
XLA Ops:
  7.3 1.3 copy.123
  8.6 2.9 collective-permute-start.7
  11.5 13.5 %collective-permute-done.7 = bf16[128,2048]{0,1:T(8,128)(2,1)S(1)} collective-permute-done((bf16[128,2048]{0,1:T(8,128)(2,1)S(1)}, bf16[128,2048]{0,1:T(8,128)(2,1)S(1)}, u32[]{:S(2)}, u32[]{:S(2)}) %collective-permute-start.7) | collective-permute-done | bytes 524320 | tf_op jit(solution)/shard_map/ppermute | solution.py:19
  25.0 3.0 collective-permute-start.8
  28.0 13.9 %collective-permute-done.8 = bf16[128,2048]{0,1:T(8,128)(2,1)S(1)} collective-permute-done((bf16[128,2048]{0,1:T(8,128)(2,1)S(1)}, bf16[128,2048]{0,1:T(8,128)(2,1)S(1)}, u32[]{:S(2)}, u32[]{:S(2)}) %collective-permute-start.8) | collective-permute-done | bytes 524320 | tf_op jit(solution)/shard_map/ppermute | solution.py:19
  41.9 1.9 collective-permute-start.9
  44.5 6.1 %collective-permute-start = (s32[128]{0:T(128)S(1)}, s32[128]{0:T(128)S(1)}, u32[]{:S(2)}, u32[]{:S(2)}) collective-permute-start(s32[128]{0:T(128)S(1)} %add_bitcast_fusion), channel_id=1, source_target_pairs={{0,1},{1,2},{2,3},{3,4},{4,5},{5,6},{6,7},{7,8},{8,9},{9,10},{10,1... | collective-permute-start | bytes 1544 | tf_op jit(solution)/shard_map/ppermute | solution.py:19
  51.3 7.5 %collective-permute-done = s32[128]{0:T(128)S(1)} collective-permute-done((s32[128]{0:T(128)S(1)}, s32[128]{0:T(128)S(1)}, u32[]{:S(2)}, u32[]{:S(2)}) %collective-permute-start) | collective-permute-done | bytes 544 | tf_op jit(solution)/shard_map/ppermute | solution.py:19
  58.8 1.9 collective-permute-start.1
  60.7 299.9 %all-gather = s32[128,4,2]{1,2,0:T(2,128)S(1)} all-gather(s32[1,4,2]{1,2,0:T(2,128)} %bitcast.282), channel_id=1, replica_groups=mesh['prompt'=4,'resp'=32] {'prompt','resp'}, dimensions={0}, use_global_device_ids=true | all-gather | bytes 4128 | tf_op jit(solution)/shard_map/all_gather | solution.py:97
  361.5 1.9 collective-permute-start.2
  363.6 3.8 sort.17
  367.4 2.4 collective-permute-start.3
  369.8 1.9 collective-permute-start.10
  371.7 3.3 collective-permute-done.3
  375.0 1.9 collective-permute-start.4
  377.6 10.7 %collective-permute-done.4 = s32[128]{0:T(128)S(1)} collective-permute-done((s32[128]{0:T(128)S(1)}, s32[128]{0:T(128)S(1)}, u32[]{:S(2)}, u32[]{:S(2)}) %collective-permute-start.4) | collective-permute-done | bytes 544 | tf_op jit(solution)/shard_map/ppermute | solution.py:19
  388.2 1.9 collective-permute-start.5
  391.4 5.0 collective-permute-done.5
  396.4 1.9 collective-permute-start.6
  398.4 3.2 copy.124
  401.6 2.6 copy.138
  404.2 1.9 collective-permute-start.11
  407.1 2.7 fusion.97
  409.8 8.6 %collective-permute-done.11 = bf16[128,2048]{0,1:T(8,128)(2,1)S(1)} collective-permute-done((bf16[128,2048]{0,1:T(8,128)(2,1)}, bf16[128,2048]{0,1:T(8,128)(2,1)S(1)}, u32[]{:S(2)}, u32[]{:S(2)}) %collective-permute-start.11) | collective-permute-done | bytes 524320 | tf_op jit(solution)/shard_map/ppermute | solution.py:19
  418.5 1.9 collective-permute-start.12
  420.4 3.3 fusion.99
  423.7 8.9 %collective-permute-done.12 = bf16[128,2048]{0,1:T(8,128)(2,1)} collective-permute-done((bf16[128,2048]{0,1:T(8,128)(2,1)S(1)}, bf16[128,2048]{0,1:T(8,128)(2,1)}, u32[]{:S(2)}, u32[]{:S(2)}) %collective-permute-start.12) | collective-permute-done | bytes 524320 | tf_op jit(solution)/shard_map/ppermute | solution.py:19
  432.7 1.9 collective-permute-start.13
  439.0 5.3 bitcast_add_fusion.8
  444.3 8.4 %conditional.8 = ((f32[128,8,8]{0,2,1:T(8,128)S(1)}, f32[128,8,8]{0,2,1:T(8,128)S(1)}, f32[128,8,8,128]{3,0,2,1:T(8,128)})) conditional(s32[]{:T(128)} %convert_element_type.71, (f32[128,8,8]{0,2,1:T(8,128)S(1)}, f32[128,8,8]{0,2,1:T(8,128)S(1)}, f32[128,8,8,128]{3,0,2,1:T(8,128)}) %tuple.61, (pred[128,128]{0,1:T(8,128)(4,1)S(1)}, ...), branch_computations={%region_9.10_spmd, %region_10.13_spmd} | conditional | flops 552615936 | bytes 25215008 | solution.py:91
  446.2 1.2 fusion.2
  447.5 5.3 bitcast_add_fusion
  452.7 8.6 %conditional.9 = ((f32[128,8,8]{0,2,1:T(8,128)S(1)}, f32[128,8,8]{0,2,1:T(8,128)S(1)}, f32[128,8,8,128]{3,0,2,1:T(8,128)})) conditional(s32[]{:T(128)} %convert_element_type.70, (f32[128,8,8]{0,2,1:T(8,128)S(1)}, f32[128,8,8]{0,2,1:T(8,128)S(1)}, f32[128,8,8,128]{3,0,2,1:T(8,128)}) %get-tuple-element.662, (pred[128,128]{0,1:T(8,128)(4,1)S(1)}, ...), branch_computations={%region_13.14_spmd, %region_14.17_spmd} | conditional | flops 552615936 | bytes 25215008 | solution.py:91
  454.8 1.2 fusion.14
  456.0 5.3 bitcast_add_fusion.1
  461.3 7.4 %conditional.10 = ((f32[128,8,8]{0,2,1:T(8,128)S(1)}, f32[128,8,8]{0,2,1:T(8,128)S(1)}, f32[128,8,8,128]{3,0,2,1:T(8,128)})) conditional(s32[]{:T(128)} %convert_element_type.69, (f32[128,8,8]{0,2,1:T(8,128)S(1)}, f32[128,8,8]{0,2,1:T(8,128)S(1)}, f32[128,8,8,128]{3,0,2,1:T(8,128)}) %get-tuple-element.663, (pred[128,128]{0,1:T(8,128)(4,1)S(1)}, ...), branch_computations={%region_17.18_spmd, %region_18.21_spmd} | conditional | flops 552615936 | bytes 25215008 | solution.py:91
  462.2 1.2 fusion.26
  463.4 5.3 bitcast_add_fusion.2
  468.7 8.5 %conditional.11 = ((f32[128,8,8]{0,2,1:T(8,128)S(1)}, f32[128,8,8]{0,2,1:T(8,128)S(1)}, f32[128,8,8,128]{3,0,2,1:T(8,128)})) conditional(s32[]{:T(128)} %convert_element_type.68, (f32[128,8,8]{0,2,1:T(8,128)S(1)}, f32[128,8,8]{0,2,1:T(8,128)S(1)}, f32[128,8,8,128]{3,0,2,1:T(8,128)}) %get-tuple-element.664, (pred[128,128]{0,1:T(8,128)(4,1)S(1)}, ...), branch_computations={%region_21.0_spmd, %region_22.25_spmd} | conditional | flops 552615936 | bytes 25215008 | solution.py:91
  470.7 1.2 fusion.38
  471.9 5.3 bitcast_add_fusion.3
  477.2 7.6 %conditional.12 = ((f32[128,8,8]{0,2,1:T(8,128)S(1)}, f32[128,8,8]{0,2,1:T(8,128)S(1)}, f32[128,8,8,128]{3,0,2,1:T(8,128)})) conditional(s32[]{:T(128)} %convert_element_type.67, (f32[128,8,8]{0,2,1:T(8,128)S(1)}, f32[128,8,8]{0,2,1:T(8,128)S(1)}, f32[128,8,8,128]{3,0,2,1:T(8,128)}) %get-tuple-element.665, (pred[128,128]{0,1:T(8,128)(4,1)S(1)}, ...), branch_computations={%region_25.0_spmd, %region_26.29_spmd} | conditional | flops 552615936 | bytes 25215008 | solution.py:91
  479.6 5.3 bitcast_add_fusion.4
  484.8 8.4 %conditional.13 = ((f32[128,8,8]{0,2,1:T(8,128)S(1)}, f32[128,8,8]{0,2,1:T(8,128)S(1)}, f32[128,8,8,128]{3,0,2,1:T(8,128)})) conditional(s32[]{:T(128)} %convert_element_type.66, (f32[128,8,8]{0,2,1:T(8,128)S(1)}, f32[128,8,8]{0,2,1:T(8,128)S(1)}, f32[128,8,8,128]{3,0,2,1:T(8,128)}) %get-tuple-element.666, (pred[128,128]{0,1:T(8,128)(4,1)S(1)}, ...), branch_computations={%region_29.30_spmd, %region_30.33_spmd} | conditional | flops 552615936 | bytes 25215008 | solution.py:91
  488.0 5.3 bitcast_add_fusion.5
  493.2 7.6 %conditional.14 = ((f32[128,8,8]{0,2,1:T(8,128)S(1)}, f32[128,8,8]{0,2,1:T(8,128)S(1)}, f32[128,8,8,128]{3,0,2,1:T(8,128)})) conditional(s32[]{:T(128)} %convert_element_type.65, (f32[128,8,8]{0,2,1:T(8,128)S(1)}, f32[128,8,8]{0,2,1:T(8,128)S(1)}, f32[128,8,8,128]{3,0,2,1:T(8,128)}) %get-tuple-element.667, (pred[128,128]{0,1:T(8,128)(4,1)S(1)}, ...), branch_computations={%region_33.34_spmd, %region_34.37_spmd} | conditional | flops 552615936 | bytes 25215008 | solution.py:91
  495.4 5.3 bitcast_add_fusion.6
  500.9 8.6 %gather_fusion.1 = bf16[128,8,2048]{2,1,0:T(8,128)(2,1)} fusion(bf16[512,8,2048]{2,1,0:T(8,128)(2,1)} %all-gather.3.cloned.1.call-done, s32[1024]{0:T(1024)S(1)} %pad_clamp_fusion), kind=kCustom, calls=%fused_computation.1 | custom fusion | bytes 8389120 | tf_op jit(solution)/shard_map/gather | solution.py:102
  509.5 6.4 %copy.137 = bf16[2,512,2048]{1,2,0:T(8,128)(2,1)} copy(bf16[2,512,2048]{2,1,0:T(8,128)(2,1)} %bitcast.261) | data formatting | bytes 8388608 | tf_op jit(solution)/shard_map/while | solution.py:127
  515.9 49.1 %while.14 = (s32[]{:T(128)}, f32[128,8,8]{0,2,1:T(8,128)S(1)}, f32[128,8,8]{0,2,1:T(8,128)S(1)}, f32[128,8,8,128]{3,0,2,1:T(8,128)}, pred[2,512]{1,0:T(4,128)(4,...) while((s32[]{:T(128)}, f32[128,8,8]{0,2,1:T(8,128)S(1)}, ...), condition=%wide.region_44.45_spmd, body=%wide.region_38.44_spmd.sunk | while | flops 2204123648 | bytes 138940144 | solution.py:127
  517.1 23.3 %conditional.16 = ((f32[128,8,8]{0,2,1:T(8,128)S(1)}, f32[128,8,8]{0,2,1:T(8,128)S(1)}, f32[128,8,8,128]{3,0,2,1:T(8,128)})) conditional(s32[]{:T(128)} %convert_element_type.97, (f32[128,8,8]{0,2,1:T(8,128)S(1)}, f32[128,8,8]{0,2,1:T(8,128)S(1)}, f32[128,8,8,128]{3,0,2,1:T(8,128)}) %tuple.148, (pred[1,512]{1,0:T(4,128)(4,1)S(1)}, ...), branch_computations={%region_40.40_spmd, %region_41.43_spmd} | conditional | flops 2204123136 | bytes 138938944 | solution.py:125
  517.2 1.7 dynamic-slice_bitcast_fusion
  519.1 4.1 bitcast_reduce_fusion
  523.2 4.9 fusion.87
  528.9 11.6 %bitcast_add_fusion.7 = f32[128,8,8,128]{3,0,2,1:T(8,128)} fusion(f32[128,8,8,128]{3,0,2,1:T(8,128)} %get-tuple-element.245, bf16[512,8,128,1]{0,2,3,1:T(8,128)(2,1)S(1)} %bitcast.260, f32[8,512,128,8]{2,1,3,0:T(8,128)} %copy-done, f32[128,8,8]{0,2,1:T(8,128)S(1)} %max.24, pred[512]{0:T(512)(128)(4,1)S(1)} %reduce.1, f32[128,8,8]{0,2,1:T(8,128)S(1)} %get-tuple-element.488), kind=kOutput, calls=%fused_computation.124 | convolution fusion | flops 1096810496 | bytes 26280448 | tf_op jit(solution)/shard_map/while/body/eval_jaxpr/cond/branch_1_fun/luem,mut->luet/dot_general | solution.py:35
  541.7 23.3 %conditional.16 = ((f32[128,8,8]{0,2,1:T(8,128)S(1)}, f32[128,8,8]{0,2,1:T(8,128)S(1)}, f32[128,8,8,128]{3,0,2,1:T(8,128)})) conditional(s32[]{:T(128)} %convert_element_type.97, (f32[128,8,8]{0,2,1:T(8,128)S(1)}, f32[128,8,8]{0,2,1:T(8,128)S(1)}, f32[128,8,8,128]{3,0,2,1:T(8,128)}) %tuple.148, (pred[1,512]{1,0:T(4,128)(4,1)S(1)}, ...), branch_computations={%region_40.40_spmd, %region_41.43_spmd} | conditional | flops 2204123136 | bytes 138938944 | solution.py:125
  541.8 1.7 dynamic-slice_bitcast_fusion
  543.6 4.1 bitcast_reduce_fusion
  547.7 4.9 fusion.87
  553.4 11.6 %bitcast_add_fusion.7 = f32[128,8,8,128]{3,0,2,1:T(8,128)} fusion(f32[128,8,8,128]{3,0,2,1:T(8,128)} %get-tuple-element.245, bf16[512,8,128,1]{0,2,3,1:T(8,128)(2,1)S(1)} %bitcast.260, f32[8,512,128,8]{2,1,3,0:T(8,128)} %copy-done, f32[128,8,8]{0,2,1:T(8,128)S(1)} %max.24, pred[512]{0:T(512)(128)(4,1)S(1)} %reduce.1, f32[128,8,8]{0,2,1:T(8,128)S(1)} %get-tuple-element.488), kind=kOutput, calls=%fused_computation.124 | convolution fusion | flops 1096810496 | bytes 26280448 | tf_op jit(solution)/shard_map/while/body/eval_jaxpr/cond/branch_1_fun/luem,mut->luet/dot_general | solution.py:35
  565.0 2.9 divide_convert_fusion
  567.9 2.7 copy.139
  570.6 4.2 convert_element_type.74
  (91 shorter events, 22.6 us)
Async XLA Ops:
  6.5 494.4 %all-gather.3.cloned.1.call-start = ((), (), s32[]{:S(2)}) async-start(), calls=%async_computation | async-start | bytes 16908288 | tf_op jit(solution)/shard_map/all_gather | solution.py:96
  8.6 16.4 %collective-permute-start.7 = (bf16[128,2048]{0,1:T(8,128)(2,1)S(1)}, bf16[128,2048]{0,1:T(8,128)(2,1)S(1)}, u32[]{:S(2)}, u32[]{:S(2)}) collective-permute-start(bf16[128,2048]{0,1:T(8,128)(2,1)S(1)} %bitcast.264), channel_id=1, source_target_pairs={{0,1},{1,2},{2,3},{3,4},{4,5},{5,6},{6,7},{7,8},{8,9},{9,10},{10,1... | collective-permute-start | bytes 1572872 | tf_op jit(solution)/shard_map/ppermute | solution.py:19
  25.0 373.3 %copy-start.5 = (bf16[128,2048]{0,1:T(8,128)(2,1)}, bf16[128,2048]{0,1:T(8,128)(2,1)S(1)}, u32[]{:S(2)}) copy-start(bf16[128,2048]{0,1:T(8,128)(2,1)S(1)} %collective-permute-done.7) | copy-start | bytes 1572868
  25.0 16.9 %collective-permute-start.8 = (bf16[128,2048]{0,1:T(8,128)(2,1)S(1)}, bf16[128,2048]{0,1:T(8,128)(2,1)S(1)}, u32[]{:S(2)}, u32[]{:S(2)}) collective-permute-start(bf16[128,2048]{0,1:T(8,128)(2,1)S(1)} %collective-permute-done.7), channel_id=1, source_target_pairs={{0,1},{1,2},{2,3},{3,4},{4,5},{5,6},{6,7},{7,8},{8,9},{9,10},{10,1... | collective-permute-start | bytes 1572872 | tf_op jit(solution)/shard_map/ppermute | solution.py:19
  41.9 356.5 %copy-start.4 = (bf16[128,2048]{0,1:T(8,128)(2,1)}, bf16[128,2048]{0,1:T(8,128)(2,1)S(1)}, u32[]{:S(2)}) copy-start(bf16[128,2048]{0,1:T(8,128)(2,1)S(1)} %collective-permute-done.8) | copy-start | bytes 1572868
  41.9 327.9 %collective-permute-start.9 = (bf16[128,2048]{0,1:T(8,128)(2,1)S(1)}, bf16[128,2048]{0,1:T(8,128)(2,1)S(1)}, u32[]{:S(2)}, u32[]{:S(2)}) collective-permute-start(bf16[128,2048]{0,1:T(8,128)(2,1)S(1)} %collective-permute-done.8), channel_id=1, source_target_pairs={{0,1},{1,2},{2,3},{3,4},{4,5},{5,6},{6,7},{7,8},{8,9},{9,10},{10,1... | collective-permute-start | bytes 1572872 | tf_op jit(solution)/shard_map/ppermute | solution.py:19
  44.5 14.3 %collective-permute-start = (s32[128]{0:T(128)S(1)}, s32[128]{0:T(128)S(1)}, u32[]{:S(2)}, u32[]{:S(2)}) collective-permute-start(s32[128]{0:T(128)S(1)} %add_bitcast_fusion), channel_id=1, source_target_pairs={{0,1},{1,2},{2,3},{3,4},{4,5},{5,6},{6,7},{7,8},{8,9},{9,10},{10,1... | collective-permute-start | bytes 1544 | tf_op jit(solution)/shard_map/ppermute | solution.py:19
  58.8 302.7 %collective-permute-start.1 = (s32[128]{0:T(128)S(1)}, s32[128]{0:T(128)S(1)}, u32[]{:S(2)}, u32[]{:S(2)}) collective-permute-start(s32[128]{0:T(128)S(1)} %collective-permute-done), channel_id=1, source_target_pairs={{0,1},{1,2},{2,3},{3,4},{4,5},{5,6},{6,7},{7,8},{8,9},{9,10},{10,1... | collective-permute-start | bytes 1544 | tf_op jit(solution)/shard_map/ppermute | solution.py:19
  361.5 5.8 %collective-permute-start.2 = (s32[128]{0:T(128)S(1)}, s32[128]{0:T(128)S(1)}, u32[]{:S(2)}, u32[]{:S(2)}) collective-permute-start(s32[128]{0:T(128)S(1)} %collective-permute-done.1), channel_id=1, source_target_pairs={{0,1},{1,2},{2,3},{3,4},{4,5},{5,6},{6,7},{7,8},{8,9},{9,10},{10,1... | collective-permute-start | bytes 1544 | tf_op jit(solution)/shard_map/ppermute | solution.py:19
  367.4 7.6 %collective-permute-start.3 = (s32[128]{0:T(128)S(1)}, s32[128]{0:T(128)S(1)}, u32[]{:S(2)}, u32[]{:S(2)}) collective-permute-start(s32[128]{0:T(128)S(1)} %collective-permute-done.2), channel_id=1, source_target_pairs={{0,1},{1,2},{2,3},{3,4},{4,5},{5,6},{6,7},{7,8},{8,9},{9,10},{10,1... | collective-permute-start | bytes 1544 | tf_op jit(solution)/shard_map/ppermute | solution.py:19
  369.8 34.4 %collective-permute-start.10 = (bf16[128,2048]{0,1:T(8,128)(2,1)S(1)}, bf16[128,2048]{0,1:T(8,128)(2,1)}, u32[]{:S(2)}, u32[]{:S(2)}) collective-permute-start(bf16[128,2048]{0,1:T(8,128)(2,1)S(1)} %collective-permute-done.9), channel_id=1, source_target_pairs={{0,1},{1,2},{2,3},{3,4},{4,5},{5,6},{6,7},{7,8},{8,9},{9,10},{10,1... | collective-permute-start | bytes 1572872 | tf_op jit(solution)/shard_map/ppermute | solution.py:19
  375.0 13.2 %collective-permute-start.4 = (s32[128]{0:T(128)S(1)}, s32[128]{0:T(128)S(1)}, u32[]{:S(2)}, u32[]{:S(2)}) collective-permute-start(s32[128]{0:T(128)S(1)} %collective-permute-done.3), channel_id=1, source_target_pairs={{0,1},{1,2},{2,3},{3,4},{4,5},{5,6},{6,7},{7,8},{8,9},{9,10},{10,1... | collective-permute-start | bytes 1544 | tf_op jit(solution)/shard_map/ppermute | solution.py:19
  388.2 8.2 %collective-permute-start.5 = (s32[128]{0:T(128)S(1)}, s32[128]{0:T(128)S(1)}, u32[]{:S(2)}, u32[]{:S(2)}) collective-permute-start(s32[128]{0:T(128)S(1)} %collective-permute-done.4), channel_id=1, source_target_pairs={{0,1},{1,2},{2,3},{3,4},{4,5},{5,6},{6,7},{7,8},{8,9},{9,10},{10,1... | collective-permute-start | bytes 1544 | tf_op jit(solution)/shard_map/ppermute | solution.py:19
  396.4 9.7 %collective-permute-start.6 = (s32[128]{0:T(128)S(1)}, s32[128]{0:T(128)S(1)}, u32[]{:S(2)}, u32[]{:S(2)}) collective-permute-start(s32[128]{0:T(128)S(1)} %collective-permute-done.5), channel_id=1, source_target_pairs={{0,1},{1,2},{2,3},{3,4},{4,5},{5,6},{6,7},{7,8},{8,9},{9,10},{10,1... | collective-permute-start | bytes 1544 | tf_op jit(solution)/shard_map/ppermute | solution.py:19
  404.2 14.3 %collective-permute-start.11 = (bf16[128,2048]{0,1:T(8,128)(2,1)}, bf16[128,2048]{0,1:T(8,128)(2,1)S(1)}, u32[]{:S(2)}, u32[]{:S(2)}) collective-permute-start(bf16[128,2048]{0,1:T(8,128)(2,1)} %collective-permute-done.10), channel_id=1, source_target_pairs={{0,1},{1,2},{2,3},{3,4},{4,5},{5,6},{6,7},{7,8},{8,9},{9,10},{10,1... | collective-permute-start | bytes 1572872 | tf_op jit(solution)/shard_map/ppermute | solution.py:19
  418.5 14.2 %copy-start.2 = (bf16[128,2048]{0,1:T(8,128)(2,1)}, bf16[128,2048]{0,1:T(8,128)(2,1)S(1)}, u32[]{:S(2)}) copy-start(bf16[128,2048]{0,1:T(8,128)(2,1)S(1)} %collective-permute-done.11) | copy-start | bytes 1572868
  418.5 14.2 %collective-permute-start.12 = (bf16[128,2048]{0,1:T(8,128)(2,1)S(1)}, bf16[128,2048]{0,1:T(8,128)(2,1)}, u32[]{:S(2)}, u32[]{:S(2)}) collective-permute-start(bf16[128,2048]{0,1:T(8,128)(2,1)S(1)} %collective-permute-done.11), channel_id=1, source_target_pairs={{0,1},{1,2},{2,3},{3,4},{4,5},{5,6},{6,7},{7,8},{8,9},{9,10},{10,1... | collective-permute-start | bytes 1572872 | tf_op jit(solution)/shard_map/ppermute | solution.py:19
  432.7 60.6 %collective-permute-start.13 = (bf16[128,2048]{0,1:T(8,128)(2,1)}, bf16[128,2048]{0,1:T(8,128)(2,1)S(1)}, u32[]{:S(2)}, u32[]{:S(2)}) collective-permute-start(bf16[128,2048]{0,1:T(8,128)(2,1)} %collective-permute-done.12), channel_id=1, source_target_pairs={{0,1},{1,2},{2,3},{3,4},{4,5},{5,6},{6,7},{7,8},{8,9},{9,10},{10,1... | collective-permute-start | bytes 1572872 | tf_op jit(solution)/shard_map/ppermute | solution.py:19
  468.7 8.5 %copy-start.3 = (bf16[128,2048]{0,1:T(8,128)(2,1)S(1)}, bf16[128,2048]{0,1:T(8,128)(2,1)}, u32[]{:S(2)}) copy-start(bf16[128,2048]{0,1:T(8,128)(2,1)} %copy-done.2) | copy-start | bytes 1572868
  509.5 6.4 %copy-start.1 = (bf16[128,8,8,128]{3,0,2,1:T(8,128)(2,1)S(1)}, bf16[128,8,8,128]{3,0,2,1:T(8,128)(2,1)}, u32[]{:S(2)}) copy-start(bf16[128,8,8,128]{3,0,2,1:T(8,128)(2,1)} %copy.138) | copy-start | bytes 6291460
  523.1 5.7 copy-start
  547.7 5.7 copy-start
Sparse Core Ops, SparseCore 0:
  9.0 354.4 all-gather.2
where the time goes:
time: 590 us; the launch traced here: 582 us
  blocking collectives  300 us (51%)
  matrix products  81.7 us (14%)
  waiting for transfers between devices  72.2 us (12%)
  local copies, waits for them, and re-layouts  41.4 us (7%)
  starting transfers between devices  33.6 us (6%)
  other arithmetic  31.8 us (5%)
  between operations  19.1 us (3%)
    all_gather x1, blocking collectives, on_device(): plan = lax.all_gather(tile_plan, ('prompt', 'resp'), axis=0, tiled=True)  300 us
    ppermute x14, waiting for transfers between devices, passed_along(): lax.ppermute(value, axis, [(source, source + steps) for source in range(f...  71.4 us
    dot_general x10, matrix products, absorb(): jnp.einsum('luem,mut->luet', attention_weight.astype(jnp.bfloat16), value...  65.2 us
    ppermute x14, starting transfers between devices, passed_along(): lax.ppermute(value, axis, [(source, source + steps) for source in range(f...  33.5 us
    reduce_sum x10, other arithmetic, absorb(): total = total * factor + jnp.sum(attention_weight, axis=-1)  21.7 us
    dot_general x10, matrix products, absorb(): jnp.einsum('wcpo,lco->wcpl', query_head_rows, key_vectors, preferred_elem...  16.5 us
  transfers between devices with their start and end apart: 15, of which 8 were waited for; matrix products, arithmetic and copies ran while one was open for 14% of the time, Pallas kernels for 0%

commit v1 on v0

v1 whole, which is shorter than its diff:
```python
import functools
import math

import jax
import jax.numpy as jnp
from jax import lax
from jax.experimental import pallas as pl
from jax.experimental.pallas import tpu as pltpu
from jax.sharding import PartitionSpec as P

H = 64
KVH = 8
HD = 128
ROWS = 128
TILE = 8
WIDE = 2 * KVH * HD
PWIDE = WIDE + 128
NEG = -1e30
C = math.log2(math.e) / math.sqrt(HD)
MESH = pl.DeviceIdType.MESH
VMEM = pltpu.VMEM
G = 8


def sort_kernel(plan_ref, prefix_ref, seg_ref, tiles_ref, seg8_ref):
    for q in range(4):
        slot = jnp.int32(0)
        place = jnp.int32(0)
        for s in range(4):
            hit = plan_ref[s, 0] == q
            slot = jnp.where(hit, s, slot)
            place = jnp.where(hit, plan_ref[s, 1], place)
        tiles_ref[q, :, :WIDE] = prefix_ref[slot]
        tiles_ref[q, :, WIDE:] = jnp.full((TILE, 128), place, jnp.int32).astype(jnp.float32).astype(jnp.bfloat16)
    seg8_ref[...] = jnp.broadcast_to(seg_ref[...], (8, 128))


def sort_tiles(plan, prefix, seg):
    return pl.pallas_call(
        sort_kernel,
        out_shape=(
            jax.ShapeDtypeStruct((4, TILE, PWIDE), jnp.bfloat16),
            jax.ShapeDtypeStruct((8, 128), jnp.int32),
        ),
        in_specs=[
            pl.BlockSpec(memory_space=pltpu.SMEM),
            pl.BlockSpec(memory_space=VMEM),
            pl.BlockSpec(memory_space=VMEM),
        ],
        out_specs=(pl.BlockSpec(memory_space=VMEM), pl.BlockSpec(memory_space=VMEM)),
        name="sort_tiles",
    )(plan, prefix, seg)


NCOPY = 64


def main_kernel(
    len_ref, q_hbm, kv_hbm, seg_hbm, tiles_hbm, out_hbm,
    q_s, rbuf, sbuf, pbuf, m_s, l_s, acc_s, bias_s, o_s,
    send, recv, local,
):
    p = lax.axis_index("prompt")
    r = lax.axis_index("resp")
    z = lax.rem(r, 2)
    x = lax.rem(r // 2, 4)
    y = r // 8

    def at(yy, xx, zz):
        return lax.rem(yy + 4, 4) * 8 + lax.rem(xx + 4, 4) * 2 + zz

    def ring(d):
        return lax.rem(r + 32 + d, 32)

    partner = r + 1 - 2 * z
    xp, xm, yp, ym = at(y, x + 1, z), at(y, x - 1, z), at(y + 1, x, z), at(y - 1, x, z)
    c1, cm1, c3, cm3 = ring(2), ring(-2), ring(6), ring(-6)
    xto = lax.rem(r + 1 + 6 * z, 32)
    xfrom = lax.rem(r + 25 + 6 * z, 32)

    barrier = pltpu.get_barrier_semaphore()
    for k in range(1, 4):
        pl.semaphore_signal(barrier, inc=1, device_id={"prompt": lax.rem(p + k, 4)}, device_id_type=MESH)
    for d in (partner, xp, xm, yp, ym, c1, cm1, c3, cm3, xto, xfrom):
        pl.semaphore_signal(barrier, inc=1, device_id={"resp": d}, device_id_type=MESH)

    l_q = pltpu.make_async_copy(q_hbm, q_s, local.at[0])
    l_kv = pltpu.make_async_copy(kv_hbm, rbuf.at[0], local.at[1])
    l_seg = pltpu.make_async_copy(seg_hbm, sbuf.at[0], local.at[2])
    l_tile = pltpu.make_async_copy(tiles_hbm.at[p], pbuf.at[r, pl.ds(pl.multiple_of(p * 8, 8), 8)], local.at[3])
    l_tile.start()
    l_kv.start()
    l_seg.start()
    l_q.start()
    pl.semaphore_wait(barrier, 14)

    counter = [0]
    started = []

    def copy(src, dst, to):
        i = counter[0]
        counter[0] += 1
        assert i < NCOPY
        c = pltpu.make_async_remote_copy(
            src_ref=src, dst_ref=dst, send_sem=send.at[i], recv_sem=recv.at[i], device_id=to, device_id_type=MESH
        )
        started.append(c)
        return c

    def rs(d):
        return {"resp": d}

    lo, hi = pl.ds(0, 64), pl.ds(64, 64)
    p0 = []
    for k in range(1, 4):
        q = lax.rem(p + k, 4)
        p0.append(copy(tiles_hbm.at[q], pbuf.at[r, pl.ds(pl.multiple_of(p * 8, 8), 8)], {"prompt": q}))
    n1 = [copy(kv_hbm.at[h], rbuf.at[1, h], rs(c1)) for h in (lo, hi)]
    n3 = [copy(kv_hbm.at[h], rbuf.at[3, h], rs(c3)) for h in (lo, hi)]
    xx = [copy(kv_hbm.at[h], rbuf.at[7, h], rs(xto)) for h in (lo, hi)]
    n2 = [copy(rbuf.at[1, lo], rbuf.at[2, lo], rs(c1)), copy(rbuf.at[3, hi], rbuf.at[2, hi], rs(cm1))]
    m1 = [copy(rbuf.at[1, h], rbuf.at[4, h], rs(partner)) for h in (lo, hi)]
    m2 = [copy(rbuf.at[2, h], rbuf.at[5, h], rs(partner)) for h in (lo, hi)]
    m3 = [copy(rbuf.at[3, h], rbuf.at[6, h], rs(partner)) for h in (lo, hi)]
    s1 = copy(seg_hbm, sbuf.at[1], rs(c1))
    s3 = copy(seg_hbm, sbuf.at[3], rs(c3))
    s7 = copy(seg_hbm, sbuf.at[7], rs(xto))
    s2 = copy(sbuf.at[1], sbuf.at[2], rs(c1))
    s4 = copy(sbuf.at[1], sbuf.at[4], rs(partner))
    s5 = copy(sbuf.at[2], sbuf.at[5], rs(partner))
    s6 = copy(sbuf.at[3], sbuf.at[6], rs(partner))

    def pair(yy, xx_):
        return pbuf.at[pl.ds(at(yy, xx_, 0), 2)]

    def one(yy, xx_, zz):
        return pbuf.at[at(yy, xx_, zz)]

    pz = copy(pbuf.at[r], pbuf.at[r], rs(partner))
    pxa = copy(pair(y, x), pair(y, x), rs(xp))
    pxb = copy(pair(y, x), pair(y, x), rs(xm))
    pxc = copy(one(y, x - 1, 0), one(y, x - 1, 0), rs(xp))
    pxd = copy(one(y, x + 1, 1), one(y, x + 1, 1), rs(xm))
    offs = (0, -1, 1, 2)
    pya = [copy(pair(y, x + o), pair(y, x + o), rs(yp)) for o in offs]
    pyb = [copy(pair(y, x + o), pair(y, x + o), rs(ym)) for o in offs]
    pyc = [copy(pair(y - 1, x + o), pair(y - 1, x + o), rs(yp)) for o in offs[:2]]
    pyd = [copy(pair(y + 1, x + o), pair(y + 1, x + o), rs(ym)) for o in offs[2:]]

    def start(*cs):
        for c in cs:
            c.start()

    def got(*cs):
        for c in cs:
            c.wait_recv()

    start(*p0, s1, s3, s7, n1[0], n3[0])
    l_tile.wait()
    got(*p0)
    start(pz, xx[0])
    got(pz)
    start(pya[0], pyb[0], pxa, pxb, n1[1], n3[1], xx[1])
    l_kv.wait()
    l_seg.wait()
    l_q.wait()

    def relay0():
        got(s1, s3)
        start(s2, s4, s6)
        got(n1[0])
        start(n2[0], m1[0])
        got(n3[0])
        start(m3[0])

    def relay1():
        got(pxa)
        start(pya[1], pyb[1], pxc)
        got(pxb)
        start(pya[2], pyb[2], pxd)

    def relay2():
        got(n1[1], n3[1])
        start(n2[1], m1[1], m3[1])
        got(s2)
        start(s5)

    def relay3():
        got(pxc, pxd)
        start(pya[3], pyb[3])
        got(pya[0], n2[0])
        start(pyc[0], m2[0])

    def relay4():
        got(pya[1], n2[1])
        start(pyc[1], m2[1])
        got(pyb[0], pyb[1], pyb[2])
        start(pyd[0])

    def relay5():
        got(pyb[3])
        start(pyd[1])

    relay0()
    relay1()
    relay2()
    relay3()
    relay4()
    relay5()

    seg_own = jnp.transpose(jnp.broadcast_to(sbuf[0, 0:1].astype(jnp.float32), (128, 128)))
    row = lax.broadcasted_iota(jnp.int32, (128, 128), 0)
    col = lax.broadcasted_iota(jnp.int32, (128, 128), 1)

    def resp_bias(slots):
        for j, s in enumerate(slots):
            if s == 0:
                d = jnp.int32(0)
            elif s <= 3:
                d = jnp.int32(2 * s)
            elif s <= 6:
                d = 2 * (s - 3) - 1 + 2 * z
            else:
                d = 7 - 6 * z
            theirs = sbuf[s, 0:1].astype(jnp.float32)
            theirs = jnp.where(r >= d, theirs, -1.0)
            ok = seg_own == theirs
            if s == 0:
                ok = ok & (col <= row)
            bias_s[:, j * 128:(j + 1) * 128] = jnp.where(ok, 0.0, NEG)

    def prefix_bias(rows):
        limit = len_ref[0]
        hot = jnp.where(lax.broadcasted_iota(jnp.int32, (8, 128), 1) == 0, 1.0, 0.0).astype(jnp.bfloat16)
        for j, yy in enumerate(rows):
            marks = pbuf[pl.ds(yy * 8, 8), :, WIDE:].reshape(256, 128)
            places = lax.dot_general(hot, marks, (((1,), (1,)), ((), ())), preferred_element_type=jnp.float32)
            tok = lax.rem(lax.broadcasted_iota(jnp.int32, (1, 256), 1), 8)
            pos = places[0:1].astype(jnp.int32) * 8 + tok
            bias_s[:, j * 256:(j + 1) * 256] = jnp.broadcast_to(jnp.where(pos < limit, 0.0, NEG), (128, 256))

    def resp_cols(slots):
        def load(off):
            return jnp.concatenate([rbuf[s, :, pl.ds(off, 128)] for s in slots], axis=0)
        return load

    def prefix_cols(rows):
        def load(off):
            return jnp.concatenate([pbuf[pl.ds(yy * 8, 8), :, pl.ds(off, 128)].reshape(256, 128) for yy in rows], axis=0)
        return load

    nt = (((1,), (1,)), ((), ()))
    nn = (((1,), (0,)), ((), ()))

    def attend(load, first, last):
        def step(h, carry):
            off = pl.multiple_of(h * 128, 128)
            k = load(off)
            v = load(pl.multiple_of(off + KVH * HD, 128))
            bias = bias_s[...]
            for g0 in range(0, 8, G):
                def cols(g):
                    return pl.ds(pl.multiple_of(off * 8 + (g0 + g) * 128, 128), 128)
                qs = jnp.concatenate([q_s[:, cols(g)] for g in range(G)], axis=0)
                scores = lax.dot_general(qs, k, nt, preferred_element_type=jnp.float32)
                ps, als, lss = [], [], []
                for g in range(G):
                    n = h * 8 + g0 + g
                    s = scores[g * 128:(g + 1) * 128] + bias
                    parts = [s[:, j * 128:(j + 1) * 128] for j in range(4)]
                    mx = jnp.max(functools.reduce(jnp.maximum, parts), axis=1, keepdims=True)
                    if first:
                        m = jnp.broadcast_to(mx, (128, 128))
                    else:
                        mo = m_s[n]
                        m = jnp.maximum(mo, mx)
                        al = jnp.exp2((mo - m) * C)
                        als.append(al)
                    w = [jnp.exp2((t - m) * C) for t in parts]
                    ls = functools.reduce(lambda a, b: a + b, w)
                    if not first:
                        ls = ls + l_s[n] * al
                    lss.append(ls)
                    if not last:
                        m_s[n] = m
                        l_s[n] = ls
                    ps.append(jnp.concatenate([t.astype(jnp.bfloat16) for t in w], axis=1))
                pv_all = lax.dot_general(jnp.concatenate(ps, axis=0), v, nn, preferred_element_type=jnp.float32)
                for g in range(G):
                    n = h * 8 + g0 + g
                    pv = pv_all[g * 128:(g + 1) * 128]
                    if not first:
                        pv = pv + acc_s[n] * als[g]
                    if not last:
                        acc_s[n] = pv
                    else:
                        tot = jnp.sum(lss[g], axis=1, keepdims=True)
                        o_s[:, cols(g)] = (pv / tot).astype(jnp.bfloat16)
            return carry
        lax.fori_loop(0, KVH, step, 0)

    ra, rb = (0, 1, 3, 7), (4, 6, 2, 5)
    y0, y1, y2, y3 = y, lax.rem(y + 3, 4), lax.rem(y + 1, 4), lax.rem(y + 2, 4)

    got(*xx, s7)
    resp_bias(ra)
    attend(resp_cols(ra), True, False)
    got(pya[2], pya[3])
    prefix_bias((y0, y1))
    attend(prefix_cols((y0, y1)), False, False)
    got(*pyc, *pyd)
    prefix_bias((y2, y3))
    attend(prefix_cols((y2, y3)), False, False)
    got(*m1, *m2, *m3, s4, s5, s6)
    resp_bias(rb)
    attend(resp_cols(rb), False, True)
    done = pltpu.make_async_copy(o_s, out_hbm, local.at[4])
    done.start()
    for c in started:
        c.wait_send()
    done.wait()


def on_device(queries, resp_kv, resp_segments, prefix_kv, tile_plan, prompt_lengths):
    tiles, seg8 = sort_tiles(tile_plan, prefix_kv, resp_segments)
    anywhere = pl.BlockSpec(memory_space=pl.ANY)
    out = pl.pallas_call(
        main_kernel,
        out_shape=jax.ShapeDtypeStruct((ROWS, H * HD), jnp.bfloat16),
        in_specs=[pl.BlockSpec(memory_space=pltpu.SMEM)] + [anywhere] * 4,
        out_specs=anywhere,
        scratch_shapes=[
            VMEM((ROWS, H * HD), jnp.bfloat16),
            VMEM((8, ROWS, WIDE), jnp.bfloat16),
            VMEM((8, 8, 128), jnp.int32),
            VMEM((32, 32, PWIDE), jnp.bfloat16),
            VMEM((H, ROWS, 128), jnp.float32),
            VMEM((H, ROWS, 128), jnp.float32),
            VMEM((H, ROWS, 128), jnp.float32),
            VMEM((ROWS, 512), jnp.float32),
            VMEM((ROWS, H * HD), jnp.bfloat16),
            pltpu.SemaphoreType.DMA((NCOPY,)),
            pltpu.SemaphoreType.DMA((NCOPY,)),
            pltpu.SemaphoreType.DMA((5,)),
        ],
        compiler_params=pltpu.CompilerParams(
            collective_id=0, has_side_effects=True, vmem_limit_bytes=60 << 20
        ),
        name="attend",
    )(prompt_lengths, queries[0], resp_kv[0], seg8, tiles)
    return out[None]


def solution(mesh):
    return jax.shard_map(
        on_device,
        mesh=mesh,
        in_specs=(
            P("prompt", "resp", None),
            P("prompt", "resp", None),
            P("prompt", "resp"),
            P(("prompt", "resp"), None, None),
            P(("prompt", "resp"), None),
            P("prompt"),
        ),
        out_specs=P("prompt", "resp", None),
        check_vma=False,
    )
```

time: 590 us -> 109 us (0.18)
  the two profiles are of different devices: /device:TPU:40 before, /device:TPU:33 now
where the time goes in v1:
time: 109 us
  Pallas kernels  104 us (95%)
  local copies, waits for them, and re-layouts  4.44 us (4%)
    pallas_call x1, Pallas kernels, on_device(): pl.pallas_call(main_kernel, out_shape=jax.ShapeDtypeStruct((ROWS, H * HD)...  103 us
    unnamed x2, local copies, waits for them, and re-layouts  4.44 us

profile of v1, /device:TPU:33, one launch (start us, length us, event | category | flops | bytes accessed | tf_op | source)
XLA Modules:
  0.0 109.2 jit_solution(5130915174828129333)
XLA Ops:
  0.7 1.3 %copy.7.plan_ref = s32[4,2]{1,0:T(4,128)} copy(s32[4,2]{0,1:T(2,128)} %param.10) | data formatting | bytes 64 | tf_op args[4]
  2.0 1.6 %sort_tiles.1 = (bf16[4,8,2176]{2,1,0:T(8,128)(2,1)}, s32[8,128]{1,0:T(8,128)}) custom-call(s32[4,2]{1,0:T(4,128)} %copy.7.plan_ref, bf16[4,8,2048]{2,1,0:T(8,128)(2,1)} %prefix_ref.1, s32[1,128]{1,0:T(1,128)} %seg_ref.1), custom_call_target="tpu_custom_call" | custom-call | tf_op jit(solution)/shard_map/sort_tiles/pallas_call | solution.py:39
  3.6 102.5 %attend.1 = bf16[128,8192]{1,0:T(8,128)(2,1)} custom-call(s32[1]{0:T(128)S(6)} %copy.9.len_ref, bf16[128,8192]{1,0:T(8,128)(2,1)} %bitcast.4, bf16[128,2048]{1,0:T(8,128)(2,1)} %bitcast.5, s32[8,128]{1,0:T(8,128)} %get-tuple-element.7.seg_hbm, bf16[4,8,2176]{2,1,0:T(8,128)(2,1)} %get-tuple-element.8.tiles_hbm), custom_call_target="tpu_custom_call" | custom-call | tf_op jit(solution)/shard_map/attend/pallas_call | solution.py:327
  106.1 3.1 %copy.10 = bf16[1,128,8192]{2,1,0:T(8,128)(2,1)} copy(bf16[1,128,8192]{2,1,0:T(8,128)(2,1)} %bitcast.3) | data formatting | bytes 4194304

commit v2 on v1

--- a/solution.py
+++ b/solution.py
@@ -27,9 +27,9 @@
         slot = jnp.int32(0)
         place = jnp.int32(0)
         for s in range(4):
-            hit = plan_ref[s, 0] == q
+            hit = plan_ref[0, s] == q
             slot = jnp.where(hit, s, slot)
-            place = jnp.where(hit, plan_ref[s, 1], place)
+            place = jnp.where(hit, plan_ref[1, s], place)
         tiles_ref[q, :, :WIDE] = prefix_ref[slot]
         tiles_ref[q, :, WIDE:] = jnp.full((TILE, 128), place, jnp.int32).astype(jnp.float32).astype(jnp.bfloat16)
     seg8_ref[...] = jnp.broadcast_to(seg_ref[...], (8, 128))
@@ -74,15 +74,15 @@
 
     partner = r + 1 - 2 * z
     xp, xm, yp, ym = at(y, x + 1, z), at(y, x - 1, z), at(y + 1, x, z), at(y - 1, x, z)
-    c1, cm1, c3, cm3 = ring(2), ring(-2), ring(6), ring(-6)
-    xto = lax.rem(r + 1 + 6 * z, 32)
-    xfrom = lax.rem(r + 25 + 6 * z, 32)
 
     barrier = pltpu.get_barrier_semaphore()
     for k in range(1, 4):
         pl.semaphore_signal(barrier, inc=1, device_id={"prompt": lax.rem(p + k, 4)}, device_id_type=MESH)
-    for d in (partner, xp, xm, yp, ym, c1, cm1, c3, cm3, xto, xfrom):
+    for d in (partner, xp, xm, yp, ym):
         pl.semaphore_signal(barrier, inc=1, device_id={"resp": d}, device_id_type=MESH)
+    for k in range(1, 8):
+        for d in (ring(k), ring(-k)):
+            pl.semaphore_signal(barrier, inc=1, device_id={"resp": d}, device_id_type=MESH)
 
     l_q = pltpu.make_async_copy(q_hbm, q_s, local.at[0])
     l_kv = pltpu.make_async_copy(kv_hbm, rbuf.at[0], local.at[1])
@@ -92,43 +92,72 @@
     l_kv.start()
     l_seg.start()
     l_q.start()
-    pl.semaphore_wait(barrier, 14)
+    l_kv.wait()
+    pl.semaphore_wait(barrier, 22)
 
     counter = [0]
     started = []
 
-    def copy(src, dst, to):
+    def copy(src, dst, to, when=None, recv_as=None):
         i = counter[0]
         counter[0] += 1
         assert i < NCOPY
         c = pltpu.make_async_remote_copy(
-            src_ref=src, dst_ref=dst, send_sem=send.at[i], recv_sem=recv.at[i], device_id=to, device_id_type=MESH
+            src_ref=src, dst_ref=dst, send_sem=send.at[i], recv_sem=recv.at[i if recv_as is None else recv_as],
+            device_id=to, device_id_type=MESH,
         )
-        started.append(c)
+        started.append((c, when))
+        c_index[id(c)] = i
         return c
+
+    c_index = {}
 
     def rs(d):
         return {"resp": d}
 
-    lo, hi = pl.ds(0, 64), pl.ds(64, 64)
+    def start(*cs, when=None):
+        def go():
+            for c in cs:
+                c.start()
+        if when is None:
+            go()
+        else:
+            pl.when(when)(go)
+
+    def got(*cs):
+        for c in cs:
+            c.wait_recv()
+
+    halves = (pl.ds(0, 64), pl.ds(64, 64))
+    OWN, ROWB = 0, 8
     p0 = []
     for k in range(1, 4):
         q = lax.rem(p + k, 4)
         p0.append(copy(tiles_hbm.at[q], pbuf.at[r, pl.ds(pl.multiple_of(p * 8, 8), 8)], {"prompt": q}))
-    n1 = [copy(kv_hbm.at[h], rbuf.at[1, h], rs(c1)) for h in (lo, hi)]
-    n3 = [copy(kv_hbm.at[h], rbuf.at[3, h], rs(c3)) for h in (lo, hi)]
-    xx = [copy(kv_hbm.at[h], rbuf.at[7, h], rs(xto)) for h in (lo, hi)]
-    n2 = [copy(rbuf.at[1, lo], rbuf.at[2, lo], rs(c1)), copy(rbuf.at[3, hi], rbuf.at[2, hi], rs(cm1))]
-    m1 = [copy(rbuf.at[1, h], rbuf.at[4, h], rs(partner)) for h in (lo, hi)]
-    m2 = [copy(rbuf.at[2, h], rbuf.at[5, h], rs(partner)) for h in (lo, hi)]
-    m3 = [copy(rbuf.at[3, h], rbuf.at[6, h], rs(partner)) for h in (lo, hi)]
-    s1 = copy(seg_hbm, sbuf.at[1], rs(c1))
-    s3 = copy(seg_hbm, sbuf.at[3], rs(c3))
-    s7 = copy(seg_hbm, sbuf.at[7], rs(xto))
-    s2 = copy(sbuf.at[1], sbuf.at[2], rs(c1))
-    s4 = copy(sbuf.at[1], sbuf.at[4], rs(partner))
-    s5 = copy(sbuf.at[2], sbuf.at[5], rs(partner))
-    s6 = copy(sbuf.at[3], sbuf.at[6], rs(partner))
+    segs = [copy(seg_hbm, sbuf.at[k], rs(ring(k))) for k in range(1, 8)]
+    src1 = jnp.where(x == 3, ROWB, OWN)
+    src3 = jnp.where(x == 0, OWN, ROWB)
+    src7 = jnp.where(z == 0, OWN, ROWB)
+    tt = [copy(rbuf.at[OWN, h], rbuf.at[ROWB, h], rs(yp)) for h in halves]
+    n1 = [copy(rbuf.at[src1, h], rbuf.at[1, h], rs(xp)) for h in halves]
+    n3 = [copy(rbuf.at[src3, h], rbuf.at[3, h], rs(xm)) for h in halves]
+    xx = [copy(rbuf.at[src7, h], rbuf.at[7, h], rs(partner)) for h in halves]
+    m1 = [copy(rbuf.at[1, h], rbuf.at[4, h], rs(partner)) for h in halves]
+    m3 = [copy(rbuf.at[3, h], rbuf.at[6, h], rs(partner)) for h in halves]
+    lo, hi = halves
+    n2 = [
+        copy(rbuf.at[1, lo], rbuf.at[2, lo], rs(xp), when=x < 3),
+        copy(rbuf.at[3, hi], rbuf.at[2, hi], rs(xm), when=x > 0),
+    ]
+    n2x = [
+        copy(rbuf.at[3, lo], rbuf.at[2, lo], rs(xm), when=x == 1, recv_as=c_index[id(n2[0])]),
+        copy(rbuf.at[1, hi], rbuf.at[2, hi], rs(xp), when=x == 2, recv_as=c_index[id(n2[1])]),
+    ]
+    m2 = [
+        copy(rbuf.at[4, lo], rbuf.at[5, lo], rs(xp), when=x < 3),
+        copy(rbuf.at[2, hi], rbuf.at[5, hi], rs(partner)),
+    ]
+    m2x = copy(rbuf.at[6, lo], rbuf.at[5, lo], rs(xm), when=x == 1, recv_as=c_index[id(m2[0])])
 
     def pair(yy, xx_):
         return pbuf.at[pl.ds(at(yy, xx_, 0), 2)]
@@ -144,76 +173,85 @@
     offs = (0, -1, 1, 2)
     pya = [copy(pair(y, x + o), pair(y, x + o), rs(yp)) for o in offs]
     pyb = [copy(pair(y, x + o), pair(y, x + o), rs(ym)) for o in offs]
-    pyc = [copy(pair(y - 1, x + o), pair(y - 1, x + o), rs(yp)) for o in offs[:2]]
-    pyd = [copy(pair(y + 1, x + o), pair(y + 1, x + o), rs(ym)) for o in offs[2:]]
-
-    def start(*cs):
-        for c in cs:
-            c.start()
-
-    def got(*cs):
-        for c in cs:
-            c.wait_recv()
-
-    start(*p0, s1, s3, s7, n1[0], n3[0])
+    pyc = copy(pair(y - 1, x), pair(y - 1, x), rs(yp))
+    pyd = [copy(pair(y + 1, x + o), pair(y + 1, x + o), rs(ym)) for o in offs[1:]]
+
+    start(*p0, tt[0])
+    start(n1[0], when=x < 3)
+    start(n3[0], when=x == 0)
+    start(*segs)
     l_tile.wait()
     got(*p0)
-    start(pz, xx[0])
+    start(pz)
+    start(xx[0], when=z == 0)
     got(pz)
-    start(pya[0], pyb[0], pxa, pxb, n1[1], n3[1], xx[1])
-    l_kv.wait()
+    start(pya[0], pyb[0], pxa, pxb, tt[1])
+    start(n1[1], when=x < 3)
+    start(n3[1], when=x == 0)
+    start(xx[1], when=z == 0)
     l_seg.wait()
     l_q.wait()
 
-    def relay0():
-        got(s1, s3)
-        start(s2, s4, s6)
-        got(n1[0])
-        start(n2[0], m1[0])
-        got(n3[0])
-        start(m3[0])
-
-    def relay1():
+    def relay_t(i):
+        got(tt[i])
+        start(n1[i], when=x == 3)
+        start(n3[i], when=x > 0)
+        start(xx[i], when=z == 1)
+
+    def relay_pa():
         got(pxa)
         start(pya[1], pyb[1], pxc)
+
+    def relay_pb():
         got(pxb)
         start(pya[2], pyb[2], pxd)
 
-    def relay2():
-        got(n1[1], n3[1])
-        start(n2[1], m1[1], m3[1])
-        got(s2)
-        start(s5)
-
-    def relay3():
+    def relay_pc():
         got(pxc, pxd)
         start(pya[3], pyb[3])
-        got(pya[0], n2[0])
-        start(pyc[0], m2[0])
-
-    def relay4():
-        got(pya[1], n2[1])
-        start(pyc[1], m2[1])
-        got(pyb[0], pyb[1], pyb[2])
-        start(pyd[0])
-
-    def relay5():
-        got(pyb[3])
-        start(pyd[1])
-
-    relay0()
-    relay1()
-    relay2()
-    relay3()
-    relay4()
-    relay5()
+
+    def relay_n1(i):
+        got(n1[i])
+        if i == 0:
+            start(n2[0], when=x < 3)
+        else:
+            start(n2x[1], when=x == 2)
+        start(m1[i])
+
+    def relay_n3(i):
+        got(n3[i])
+        if i == 0:
+            start(n2x[0], when=x == 1)
+        else:
+            start(n2[1], when=x > 0)
+        start(m3[i])
+
+    def relay_m1():
+        got(m1[0])
+        start(m2[0], when=x < 3)
+
+    def relay_m3():
+        got(m3[0])
+        start(m2x, when=x == 1)
+
+    def relay_n2():
+        got(n2[1])
+        start(m2[1])
+
+    def relay_yc():
+        got(pya[0])
+        start(pyc)
+
+    def relay_yd(i):
+        got(pyb[1 + i])
+        start(pyd[i])
 
     seg_own = jnp.transpose(jnp.broadcast_to(sbuf[0, 0:1].astype(jnp.float32), (128, 128)))
     row = lax.broadcasted_iota(jnp.int32, (128, 128), 0)
     col = lax.broadcasted_iota(jnp.int32, (128, 128), 1)
 
     def resp_bias(slots):
-        for j, s in enumerate(slots):
+        for j, s in slots:
             if s == 0:
                 d = jnp.int32(0)
             elif s <= 3:
@@ -222,7 +260,7 @@
                 d = 2 * (s - 3) - 1 + 2 * z
             else:
                 d = 7 - 6 * z
-            theirs = sbuf[s, 0:1].astype(jnp.float32)
+            theirs = sbuf[d, 0:1].astype(jnp.float32)
             theirs = jnp.where(r >= d, theirs, -1.0)
             ok = seg_own == theirs
             if s == 0:
@@ -232,12 +270,12 @@
     def prefix_bias(rows):
         limit = len_ref[0]
         hot = jnp.where(lax.broadcasted_iota(jnp.int32, (8, 128), 1) == 0, 1.0, 0.0).astype(jnp.bfloat16)
-        for j, yy in enumerate(rows):
+        for j, yy in rows:
             marks = pbuf[pl.ds(yy * 8, 8), :, WIDE:].reshape(256, 128)
             places = lax.dot_general(hot, marks, (((1,), (1,)), ((), ())), preferred_element_type=jnp.float32)
             tok = lax.rem(lax.broadcasted_iota(jnp.int32, (1, 256), 1), 8)
             pos = places[0:1].astype(jnp.int32) * 8 + tok
-            bias_s[:, j * 256:(j + 1) * 256] = jnp.broadcast_to(jnp.where(pos < limit, 0.0, NEG), (128, 256))
+            bias_s[:, j * 128:j * 128 + 256] = jnp.broadcast_to(jnp.where(pos < limit, 0.0, NEG), (128, 256))
 
     def resp_cols(slots):
         def load(off):
@@ -252,12 +290,17 @@
     nt = (((1,), (1,)), ((), ()))
     nn = (((1,), (0,)), ((), ()))
 
-    def attend(load, first, last):
+    def attend(load, width, first, last, hooks=()):
         def step(h, carry):
+            for i, fns in hooks:
+                def run(fns=fns):
+                    for f in fns:
+                        f()
+                pl.when(h == i)(run)
             off = pl.multiple_of(h * 128, 128)
             k = load(off)
             v = load(pl.multiple_of(off + KVH * HD, 128))
-            bias = bias_s[...]
+            bias = bias_s[:, :width * 128]
             for g0 in range(0, 8, G):
                 def cols(g):
                     return pl.ds(pl.multiple_of(off * 8 + (g0 + g) * 128, 128), 128)
@@ -267,7 +310,7 @@
                 for g in range(G):
                     n = h * 8 + g0 + g
                     s = scores[g * 128:(g + 1) * 128] + bias
-                    parts = [s[:, j * 128:(j + 1) * 128] for j in range(4)]
+                    parts = [s[:, j * 128:(j + 1) * 128] for j in range(width)]
                     mx = jnp.max(functools.reduce(jnp.maximum, parts), axis=1, keepdims=True)
                     if first:
                         m = jnp.broadcast_to(mx, (128, 128))
@@ -299,30 +342,56 @@
             return carry
         lax.fori_loop(0, KVH, step, 0)
 
-    ra, rb = (0, 1, 3, 7), (4, 6, 2, 5)
     y0, y1, y2, y3 = y, lax.rem(y + 3, 4), lax.rem(y + 1, 4), lax.rem(y + 2, 4)
 
-    got(*xx, s7)
-    resp_bias(ra)
-    attend(resp_cols(ra), True, False)
-    got(pya[2], pya[3])
-    prefix_bias((y0, y1))
-    attend(prefix_cols((y0, y1)), False, False)
-    got(*pyc, *pyd)
-    prefix_bias((y2, y3))
-    attend(prefix_cols((y2, y3)), False, False)
-    got(*m1, *m2, *m3, s4, s5, s6)
-    resp_bias(rb)
-    attend(resp_cols(rb), False, True)
+    def both(slots, rows):
+        loads = [resp_cols(slots)] if slots else []
+        loads += [prefix_cols(rows)] if rows else []
+        def load(off):
+            return jnp.concatenate([f(off) for f in loads], axis=0) if len(loads) > 1 else loads[0](off)
+        resp_bias(list(enumerate(slots)))
+        prefix_bias([(len(slots) + 2 * i, yy) for i, yy in enumerate(rows)])
+        return load, len(slots) + 2 * len(rows)
+
+    relay_t(0)
+    relay_pa()
+    relay_pb()
+    relay_n1(0)
+    relay_t(1)
+    relay_pc()
+    load, width = both((0,), (y0,))
+    attend(load, width, True, False, hooks=(
+        (0, (lambda: relay_n3(0), lambda: relay_n1(1))),
+        (2, (relay_yc, relay_m1)),
+        (4, (lambda: relay_n3(1), lambda: relay_yd(0))),
+        (6, (lambda: got(*xx, *segs), lambda: relay_yd(1), relay_m3)),
+    ))
+    load, width = both((1, 3, 7), ())
+    attend(load, width, False, False, hooks=(
+        (1, (relay_n2,)),
+        (4, (lambda: relay_yd(2),)),
+    ))
+    got(*pya[1:], pyb[0])
+    load, width = both((), (y1, y2))
+    attend(load, width, False, False)
+    got(m1[1], m3[1], n2[0])
+    load, width = both((4, 6, 2), ())
+    attend(load, width, False, False)
+    got(pyc, *pyd, *m2)
+    load, width = both((5,), (y3,))
+    attend(load, width, False, True)
     done = pltpu.make_async_copy(o_s, out_hbm, local.at[4])
     done.start()
-    for c in started:
-        c.wait_send()
+    for c, when in started:
+        if when is None:
+            c.wait_send()
+        else:
+            pl.when(when)(c.wait_send)
     done.wait()
 
 
 def on_device(queries, resp_kv, resp_segments, prefix_kv, tile_plan, prompt_lengths):
-    tiles, seg8 = sort_tiles(tile_plan, prefix_kv, resp_segments)
+    tiles, seg8 = sort_tiles(tile_plan.T, prefix_kv, resp_segments)
     anywhere = pl.BlockSpec(memory_space=pl.ANY)
     out = pl.pallas_call(
         main_kernel,
@@ -331,7 +400,7 @@
         out_specs=anywhere,
         scratch_shapes=[
             VMEM((ROWS, H * HD), jnp.bfloat16),
-            VMEM((8, ROWS, WIDE), jnp.bfloat16),
+            VMEM((9, ROWS, WIDE), jnp.bfloat16),
             VMEM((8, 8, 128), jnp.int32),
             VMEM((32, 32, PWIDE), jnp.bfloat16),
             VMEM((H, ROWS, 128), jnp.float32),

time: 109 us -> 88.3 us (0.81)
  the two profiles are of different devices: /device:TPU:33 before, /device:TPU:0 now
where the time goes in v2:
time: 88.3 us; the launch traced here: 88.1 us
  Pallas kernels  84.4 us (96%)
  local copies, waits for them, and re-layouts  3.1 us (4%)
    pallas_call x1, Pallas kernels, on_device(): pl.pallas_call(main_kernel, out_shape=jax.ShapeDtypeStruct((ROWS, H * HD)...  82.8 us
    unnamed x1, local copies, waits for them, and re-layouts  3.1 us

profile of v2, /device:TPU:0, one launch (start us, length us, event | category | flops | bytes accessed | tf_op | source)
XLA Modules:
  0.0 88.1 jit_solution(813881275865930657)
XLA Ops:
  0.7 1.6 %sort_tiles.1 = (bf16[4,8,2176]{2,1,0:T(8,128)(2,1)}, s32[8,128]{1,0:T(8,128)}) custom-call(s32[2,4]{1,0:T(2,128)} %bitcast.7, bf16[4,8,2048]{2,1,0:T(8,128)(2,1)} %prefix_ref.1, s32[1,128]{1,0:T(1,128)} %seg_ref.1), custom_call_target="tpu_custom_call" | custom-call | tf_op jit(solution)/shard_map/sort_tiles/pallas_call | solution.py:39
  2.3 82.8 %attend.1 = bf16[128,8192]{1,0:T(8,128)(2,1)} custom-call(s32[1]{0:T(128)S(6)} %copy.8.len_ref, bf16[128,8192]{1,0:T(8,128)(2,1)} %bitcast.5, bf16[128,2048]{1,0:T(8,128)(2,1)} %bitcast.6, s32[8,128]{1,0:T(8,128)} %get-tuple-element.7.seg_hbm, bf16[4,8,2176]{2,1,0:T(8,128)(2,1)} %get-tuple-element.8.tiles_hbm), custom_call_target="tpu_custom_call" | custom-call | tf_op jit(solution)/shard_map/attend/pallas_call | solution.py:396
  85.0 3.1 %copy.9 = bf16[1,128,8192]{2,1,0:T(8,128)(2,1)} copy(bf16[1,128,8192]{2,1,0:T(8,128)(2,1)} %bitcast.4) | data formatting | bytes 4194304

commit v3 on v2

--- a/solution.py
+++ b/solution.py
@@ -77,7 +77,9 @@
 
     barrier = pltpu.get_barrier_semaphore()
     for k in range(1, 4):
-        pl.semaphore_signal(barrier, inc=1, device_id={"prompt": lax.rem(p + k, 4)}, device_id_type=MESH)
+        q = lax.rem(p + k, 4)
+        pl.semaphore_signal(barrier, inc=1, device_id={"prompt": q}, device_id_type=MESH)
+        pl.semaphore_signal(barrier, inc=1, device_id={"prompt": q, "resp": partner}, device_id_type=MESH)
     for d in (partner, xp, xm, yp, ym):
         pl.semaphore_signal(barrier, inc=1, device_id={"resp": d}, device_id_type=MESH)
     for k in range(1, 8):
@@ -93,7 +95,7 @@
     l_seg.start()
     l_q.start()
     l_kv.wait()
-    pl.semaphore_wait(barrier, 22)
+    pl.semaphore_wait(barrier, 25)
 
     counter = [0]
     started = []
@@ -124,16 +126,25 @@
         else:
             pl.when(when)(go)
 
+    waited = set()
+
     def got(*cs):
         for c in cs:
-            c.wait_recv()
+            if id(c) not in waited:
+                waited.add(id(c))
+                c.wait_recv()
 
     halves = (pl.ds(0, 64), pl.ds(64, 64))
     OWN, ROWB = 0, 8
+    def tile_at():
+        return pbuf.at[r, pl.ds(pl.multiple_of(p * 8, 8), 8)]
+
     p0 = []
     for k in range(1, 4):
         q = lax.rem(p + k, 4)
-        p0.append(copy(tiles_hbm.at[q], pbuf.at[r, pl.ds(pl.multiple_of(p * 8, 8), 8)], {"prompt": q}))
+        p0.append(copy(tiles_hbm.at[q], tile_at(), {"prompt": q}))
+        p0.append(copy(tiles_hbm.at[q], tile_at(), {"prompt": q, "resp": partner}))
+    p0.append(copy(tiles_hbm.at[p], tile_at(), rs(partner)))
     segs = [copy(seg_hbm, sbuf.at[k], rs(ring(k))) for k in range(1, 8)]
     src1 = jnp.where(x == 3, ROWB, OWN)
     src3 = jnp.where(x == 0, OWN, ROWB)
@@ -165,7 +176,6 @@
     def one(yy, xx_, zz):
         return pbuf.at[at(yy, xx_, zz)]
 
-    pz = copy(pbuf.at[r], pbuf.at[r], rs(partner))
     pxa = copy(pair(y, x), pair(y, x), rs(xp))
     pxb = copy(pair(y, x), pair(y, x), rs(xm))
     pxc = copy(one(y, x - 1, 0), one(y, x - 1, 0), rs(xp))
@@ -173,24 +183,32 @@
     offs = (0, -1, 1, 2)
     pya = [copy(pair(y, x + o), pair(y, x + o), rs(yp)) for o in offs]
     pyb = [copy(pair(y, x + o), pair(y, x + o), rs(ym)) for o in offs]
-    pyc = copy(pair(y - 1, x), pair(y - 1, x), rs(yp))
-    pyd = [copy(pair(y + 1, x + o), pair(y + 1, x + o), rs(ym)) for o in offs[1:]]
-
-    start(*p0, tt[0])
+    pyc = [
+        copy(pair(y - 1, x), pair(y - 1, x), rs(yp)),
+        copy(one(y - 1, x + 1, 0), one(y - 1, x + 1, 0), rs(yp)),
+    ]
+    pyd = [
+        copy(one(y + 1, x + 1, 1), one(y + 1, x + 1, 1), rs(ym)),
+        copy(pair(y + 1, x - 1), pair(y + 1, x - 1), rs(ym)),
+        copy(pair(y + 1, x + 2), pair(y + 1, x + 2), rs(ym)),
+    ]
+
+    start(*p0, *tt)
     start(n1[0], when=x < 3)
     start(n3[0], when=x == 0)
+    start(*xx, when=z == 0)
     start(*segs)
     l_tile.wait()
     got(*p0)
-    start(pz)
-    start(xx[0], when=z == 0)
-    got(pz)
-    start(pya[0], pyb[0], pxa, pxb, tt[1])
+    start(pxa, pxb, pyb[0], pya[0])
     start(n1[1], when=x < 3)
     start(n3[1], when=x == 0)
-    start(xx[1], when=z == 0)
     l_seg.wait()
     l_q.wait()
+
+    def got_if(cond, c):
+        waited.add(id(c))
+        pl.when(cond)(c.wait_recv)
 
     def relay_t(i):
         got(tt[i])
@@ -200,23 +218,34 @@
 
     def relay_pa():
         got(pxa)
-        start(pya[1], pyb[1], pxc)
+        start(pxc, pyb[1], pya[1])
 
     def relay_pb():
         got(pxb)
-        start(pya[2], pyb[2], pxd)
+        start(pxd, pyb[2], pya[2])
 
     def relay_pc():
         got(pxc, pxd)
-        start(pya[3], pyb[3])
-
-    def relay_n1(i):
-        got(n1[i])
+        start(pyb[3], pya[3])
+
+    def take_n1(i, cond):
+        got_if(cond, n1[i])
+        start(m1[i], when=cond)
+
+    late = set()
+
+    def late_n1(i):
+        if i not in late:
+            late.add(i)
+            take_n1(i, x == 0)
+            if i == 0:
+                start(n2[0], when=x == 0)
+
+    def send_n2(i):
         if i == 0:
             start(n2[0], when=x < 3)
         else:
             start(n2x[1], when=x == 2)
-        start(m1[i])
 
     def relay_n3(i):
         got(n3[i])
@@ -238,13 +267,55 @@
         got(n2[1])
         start(m2[1])
 
-    def relay_yc():
-        got(pya[0])
-        start(pyc)
-
-    def relay_yd(i):
-        got(pyb[1 + i])
-        start(pyd[i])
+    def relay_ya(i):
+        got(pya[i])
+        if i == 0:
+            start(pyc[0])
+        if i == 2:
+            start(pyc[1])
+
+    def relay_yb(i):
+        got(pyb[i])
+        if i == 2:
+            start(pyd[0])
+        if i == 1:
+            start(pyd[1])
+        if i == 3:
+            start(pyd[2])
+
+    relays = [
+        (11.5, lambda: relay_t(0)),
+        (12, lambda: take_n1(0, x > 0)),
+        (17, lambda: relay_pb()),
+        (17.2, lambda: relay_pa()),
+        (17.5, lambda: relay_t(1)),
+        (17.6, lambda: pl.when(x > 0)(lambda: send_n2(0))),
+        (22, lambda: relay_n3(0)),
+        (22.6, lambda: late_n1(0)),
+        (23, lambda: relay_ya(0)),
+        (24, lambda: take_n1(1, x > 0)),
+        (25.8, lambda: relay_pc()),
+        (25.9, lambda: send_n2(1)),
+        (26, lambda: relay_yb(2)),
+        (29, lambda: relay_ya(2)),
+        (29.5, lambda: late_n1(1)),
+        (31, lambda: relay_m1()),
+        (31.5, lambda: relay_n3(1)),
+        (32, lambda: relay_yb(1)),
+        (37.5, lambda: relay_yb(3)),
+        (38, lambda: relay_n2()),
+        (38.5, lambda: relay_m3()),
+    ]
+
+    def due(t):
+        fns = []
+        while relays and relays[0][0] <= t:
+            fns.append(relays.pop(0)[1])
+        return fns
+
+    def relay_until(t):
+        for f in due(t):
+            f()
 
     seg_own = jnp.transpose(jnp.broadcast_to(sbuf[0, 0:1].astype(jnp.float32), (128, 128)))
     row = lax.broadcasted_iota(jnp.int32, (128, 128), 0)
@@ -267,30 +338,37 @@
                 ok = ok & (col <= row)
             bias_s[:, j * 128:(j + 1) * 128] = jnp.where(ok, 0.0, NEG)
 
-    def prefix_bias(rows):
+    def tiles_of(yy, part, lanes):
+        xs = ((x, x - 1), (x + 1, x + 2))[part]
+        return jnp.concatenate([pbuf[pl.ds(at(yy, c, 0), 2), :, lanes].reshape(64, 128) for c in xs], axis=0)
+
+    def prefix_bias(halves_):
         limit = len_ref[0]
         hot = jnp.where(lax.broadcasted_iota(jnp.int32, (8, 128), 1) == 0, 1.0, 0.0).astype(jnp.bfloat16)
-        for j, yy in rows:
-            marks = pbuf[pl.ds(yy * 8, 8), :, WIDE:].reshape(256, 128)
+        for j, (yy, part) in halves_:
+            marks = tiles_of(yy, part, pl.ds(WIDE, 128))
             places = lax.dot_general(hot, marks, (((1,), (1,)), ((), ())), preferred_element_type=jnp.float32)
-            tok = lax.rem(lax.broadcasted_iota(jnp.int32, (1, 256), 1), 8)
+            tok = lax.rem(lax.broadcasted_iota(jnp.int32, (1, 128), 1), 8)
             pos = places[0:1].astype(jnp.int32) * 8 + tok
-            bias_s[:, j * 128:j * 128 + 256] = jnp.broadcast_to(jnp.where(pos < limit, 0.0, NEG), (128, 256))
+            bias_s[:, j * 128:(j + 1) * 128] = jnp.broadcast_to(jnp.where(pos < limit, 0.0, NEG), (128, 128))
 
     def resp_cols(slots):
         def load(off):
             return jnp.concatenate([rbuf[s, :, pl.ds(off, 128)] for s in slots], axis=0)
         return load
 
-    def prefix_cols(rows):
+    def prefix_cols(halves_):
         def load(off):
-            return jnp.concatenate([pbuf[pl.ds(yy * 8, 8), :, pl.ds(off, 128)].reshape(256, 128) for yy in rows], axis=0)
+            return jnp.concatenate([tiles_of(yy, part, pl.ds(off, 128)) for yy, part in halves_], axis=0)
         return load
 
     nt = (((1,), (1,)), ((), ()))
     nn = (((1,), (0,)), ((), ()))
 
-    def attend(load, width, first, last, hooks=()):
+    def attend(load, width, first, last, t0, dt):
+        hooks = [(i, due(t0 + i * dt)) for i in range(KVH)]
+        hooks = [(i, fns) for i, fns in hooks if fns]
+
         def step(h, carry):
             for i, fns in hooks:
                 def run(fns=fns):
@@ -342,44 +420,48 @@
             return carry
         lax.fori_loop(0, KVH, step, 0)
 
-    y0, y1, y2, y3 = y, lax.rem(y + 3, 4), lax.rem(y + 1, 4), lax.rem(y + 2, 4)
-
-    def both(slots, rows):
+    def both(slots, halves_):
         loads = [resp_cols(slots)] if slots else []
-        loads += [prefix_cols(rows)] if rows else []
+        loads += [prefix_cols(halves_)] if halves_ else []
         def load(off):
             return jnp.concatenate([f(off) for f in loads], axis=0) if len(loads) > 1 else loads[0](off)
         resp_bias(list(enumerate(slots)))
-        prefix_bias([(len(slots) + 2 * i, yy) for i, yy in enumerate(rows)])
-        return load, len(slots) + 2 * len(rows)
-
-    relay_t(0)
-    relay_pa()
-    relay_pb()
-    relay_n1(0)
-    relay_t(1)
-    relay_pc()
-    load, width = both((0,), (y0,))
-    attend(load, width, True, False, hooks=(
-        (0, (lambda: relay_n3(0), lambda: relay_n1(1))),
-        (2, (relay_yc, relay_m1)),
-        (4, (lambda: relay_n3(1), lambda: relay_yd(0))),
-        (6, (lambda: got(*xx, *segs), lambda: relay_yd(1), relay_m3)),
-    ))
-    load, width = both((1, 3, 7), ())
-    attend(load, width, False, False, hooks=(
-        (1, (relay_n2,)),
-        (4, (lambda: relay_yd(2),)),
-    ))
-    got(*pya[1:], pyb[0])
-    load, width = both((), (y1, y2))
-    attend(load, width, False, False)
-    got(m1[1], m3[1], n2[0])
-    load, width = both((4, 6, 2), ())
-    attend(load, width, False, False)
-    got(pyc, *pyd, *m2)
-    load, width = both((5,), (y3,))
-    attend(load, width, False, True)
+        prefix_bias([(len(slots) + i, half) for i, half in enumerate(halves_)])
+        return load, len(slots) + len(halves_)
+
+    ready = {0: (), 1: n1, 2: n2, 3: n3, 4: m1, 5: m2, 6: m3, 7: xx}
+
+    def need(slots, halves_):
+        for s in slots:
+            if s == 1:
+                late_n1(0)
+                late_n1(1)
+            got(*ready[s])
+        if any(slots):
+            got(*segs)
+        for d, part in halves_:
+            if d == 0:
+                got(*((pxa,), (pxb, pxc, pxd))[part])
+            elif d == -1:
+                got(*((pya[0], pya[1]), (pya[2], pya[3]))[part])
+            elif d == 1:
+                got(*((pyb[0], pyb[1]), (pyb[2], pyb[3]))[part])
+            else:
+                got(*((pyc[0], pyd[1]), (pyc[1], pyd[0], pyd[2]))[part])
+
+    def chunk(t0, dt, slots, halves_, first=False, last=False):
+        relay_until(t0)
+        need(slots, halves_)
+        load, width = both(slots, [(y + d, part) for d, part in halves_])
+        attend(load, width, first, last, t0, dt)
+
+    chunk(10, 0.4, (0,), (), first=True)
+    chunk(18, 0.6, (), ((0, 0),))
+    chunk(27, 0.85, (1, 7), ((0, 1), (1, 0)))
+    chunk(35, 0.95, (3, 4), ((-1, 0),))
+    chunk(42, 0.9, (2,), ((1, 1), (-1, 1)))
+    relay_until(100)
+    chunk(50, 0.9, (6, 5), ((2, 0), (2, 1)), last=True)
     done = pltpu.make_async_copy(o_s, out_hbm, local.at[4])
     done.start()
     for c, when in started:
@@ -406,7 +488,7 @@
             VMEM((H, ROWS, 128), jnp.float32),
             VMEM((H, ROWS, 128), jnp.float32),
             VMEM((H, ROWS, 128), jnp.float32),
-            VMEM((ROWS, 512), jnp.float32),
+            VMEM((ROWS, 640), jnp.float32),
             VMEM((ROWS, H * HD), jnp.bfloat16),
             pltpu.SemaphoreType.DMA((NCOPY,)),
             pltpu.SemaphoreType.DMA((NCOPY,)),

time: 88.3 us -> 76 us (0.86)
  Pallas kernels: 84.4 us -> 72.1 us
    pallas_call x1, Pallas kernels: 82.8 us -> 70.5 us  [on_device(): pl.pallas_call(main_kernel, out_shape=jax.ShapeDtypeStruct((ROWS, H * HD)...]
where the time goes in v3:
time: 76 us; the launch traced here: 75.9 us
  Pallas kernels  72.1 us (95%)
  local copies, waits for them, and re-layouts  3.1 us (4%)
    pallas_call x1, Pallas kernels, on_device(): pl.pallas_call(main_kernel, out_shape=jax.ShapeDtypeStruct((ROWS, H * HD)...  70.5 us
    unnamed x1, local copies, waits for them, and re-layouts  3.1 us
    pallas_call x1, Pallas kernels, sort_tiles(): pl.pallas_call(sort_kernel, out_shape=(jax.ShapeDtypeStruct((4, TILE, PWI...  1.6 us

profile of v3, /device:TPU:0, one launch (start us, length us, event | category | flops | bytes accessed | tf_op | source)
XLA Modules:
  0.0 75.9 jit_solution(11608618948099603388)
XLA Ops:
  0.7 1.6 %sort_tiles.1 = (bf16[4,8,2176]{2,1,0:T(8,128)(2,1)}, s32[8,128]{1,0:T(8,128)}) custom-call(s32[2,4]{1,0:T(2,128)} %bitcast.7, bf16[4,8,2048]{2,1,0:T(8,128)(2,1)} %prefix_ref.1, s32[1,128]{1,0:T(1,128)} %seg_ref.1), custom_call_target="tpu_custom_call" | custom-call | tf_op jit(solution)/shard_map/sort_tiles/pallas_call | solution.py:39
  2.3 70.5 %attend.1 = bf16[128,8192]{1,0:T(8,128)(2,1)} custom-call(s32[1]{0:T(128)S(6)} %copy.8.len_ref, bf16[128,8192]{1,0:T(8,128)(2,1)} %bitcast.5, bf16[128,2048]{1,0:T(8,128)(2,1)} %bitcast.6, s32[8,128]{1,0:T(8,128)} %get-tuple-element.7.seg_hbm, bf16[4,8,2176]{2,1,0:T(8,128)(2,1)} %get-tuple-element.8.tiles_hbm), custom_call_target="tpu_custom_call" | custom-call | tf_op jit(solution)/shard_map/attend/pallas_call | solution.py:478
  72.8 3.1 %copy.9 = bf16[1,128,8192]{2,1,0:T(8,128)(2,1)} copy(bf16[1,128,8192]{2,1,0:T(8,128)(2,1)} %bitcast.4) | data formatting | bytes 4194304
